TPU v7x, 512 devices: a whole 4x8x8 slice. The times are simulated.
512 devices in a mesh: tm: 16 (over y, core), vert: 32 (over x, z).
Axes of the slice: x: 4, y: 8, z: 8, core: 2. Of those that a mesh axis runs over, the one named last changes fastest.
Arguments:
- features: bfloat16 [16, 16384, 1024], P('tm', 'vert'), may hold values from -6 to 6
- graph_weight: bfloat16 [1024, 1024], P('vert'), may hold values from -0.1875 to 0.1875
- head_weight: bfloat16 [16, 192, 1024], P('tm'), may hold values from -16 to 16
- send_rows: int32 [16, 32, 32, 16], P('tm', 'vert'), may hold values from 0 to 511, as said below
- send_count: int32 [16, 32, 32], P('tm', 'vert'), may hold values from 0 to 16, as said below
- block_index: int32 [16, 128, 3], P('tm', 'vert'), may hold values from 0 to 7, as said below
- block_values: bfloat16 [16, 16384, 3, 128], P('tm', 'vert'), may hold values from -0.3125 to 0.3125
Outputs:
- combined: bfloat16 [16, 16384, 1024], P('tm', 'vert')
Inputs may be any that keep to these rules, and one draw needn't show every extreme that they name: send_rows[s, p, q] holds 16 distinct local rows of partition p; slots from send_count[s, p, q] on are ignored. send_count[s, p, p] is 0; in every snapshot some pairs reach 16. `block_index`: the 3 entries of a block row are distinct; column blocks below 4 are the partition's own rows, the others its boundary rows in the order of columns.
All inputs are finite; a program needn't handle non-finite values.
Results may differ from a plain program's by a relative error of at most 0.0075.
Values may be sent and summed in bfloat16 or wider, within the bound.
A program may use at most 64 MiB of HBM per device.

v0:
```python
import jax
import jax.numpy as jnp
from jax import lax
from jax.sharding import PartitionSpec as P


def attend_heads(regrouped, head_piece):
    head_size = head_piece.shape[1] // 3
    count_heads = head_piece.shape[0]
    snapshots = regrouped.shape[0]
    packed = jnp.einsum("tvd,hcd->tvhc", regrouped, head_piece, preferred_element_type=jnp.float32)
    queries = packed[..., :head_size].astype(jnp.bfloat16)
    keys_part = packed[..., head_size : 2 * head_size].astype(jnp.bfloat16)
    values = packed[..., 2 * head_size :].astype(jnp.bfloat16)
    scores = jnp.einsum(
        "tvhc,svhc->vhts", queries, keys_part, preferred_element_type=jnp.float32
    ) * head_size ** (-0.5)
    causal = jnp.arange(snapshots)[:, None] >= jnp.arange(snapshots)[None, :]
    scores = jnp.where(causal, scores, -1e30)
    row_max = jnp.max(scores, axis=-1, keepdims=True)
    exponent = jnp.where(causal, jnp.exp(scores - row_max), 0.0)
    attention = (exponent / jnp.sum(exponent, axis=-1, keepdims=True)).astype(jnp.bfloat16)
    attended = jnp.einsum("vhts,svhc->tvhc", attention, values, preferred_element_type=jnp.float32)
    return attended.astype(jnp.bfloat16).reshape(
        snapshots, regrouped.shape[1], count_heads * head_size
    )


def fold_rows(left, piece):
    return jnp.dot(left, piece, preferred_element_type=jnp.float32)


def shards(features, graph_weight, head_weight, send_rows, send_count, block_index, block_values):
    inputs = features[0]
    feature_width = inputs.shape[1]
    own_count = inputs.shape[0]
    rows_list = send_rows[0, 0]
    sources = rows_list.shape[0]
    most_rows = rows_list.shape[1]
    live_slots = jnp.arange(most_rows)[None, :] < send_count[0, 0][:, None]
    projected = fold_rows(inputs, lax.all_gather(graph_weight, "vert", axis=0, tiled=True)).astype(
        jnp.bfloat16
    )
    picked = jnp.take(projected, rows_list.reshape(-1), axis=0).reshape(
        sources, most_rows, feature_width
    )
    picked = jnp.where(live_slots[:, :, None], picked, jnp.zeros_like(picked))
    received = lax.all_to_all(picked, "vert", split_axis=0, concat_axis=0, tiled=True)
    block_size = block_values.shape[-1]
    index_list = block_index[0]
    own_blocks = index_list.shape[0]
    chosen_count = index_list.shape[1]
    columns = jnp.concatenate(
        [projected, received.reshape(sources * most_rows, feature_width)], axis=0
    )
    columns = columns.reshape(-1, block_size, feature_width)
    chosen = jnp.take(columns, index_list.reshape(-1), axis=0).reshape(
        own_blocks, chosen_count, block_size, feature_width
    )
    edge_weights = block_values[0].reshape(own_blocks, block_size, chosen_count, block_size)
    summed = jnp.einsum("rikj,rkjd->rid", edge_weights, chosen, preferred_element_type=jnp.float32)
    pre_act = projected.astype(jnp.float32) + summed.reshape(own_count, feature_width)
    hidden = jax.nn.relu(pre_act).astype(jnp.bfloat16)
    regrouped = lax.all_to_all(hidden[None], "tm", split_axis=1, concat_axis=0, tiled=True)
    attended = attend_heads(regrouped, lax.all_gather(head_weight, "tm", axis=0, tiled=True))
    returned = lax.all_to_all(attended, "tm", split_axis=0, concat_axis=1, tiled=True)
    combined = (hidden.astype(jnp.float32) + returned[0].astype(jnp.float32)).astype(jnp.bfloat16)
    return combined[None]


def solution(mesh):
    return jax.shard_map(
        shards,
        mesh=mesh,
        in_specs=(
            P("tm", "vert", None),
            P("vert", None),
            P("tm", None, None),
            P("tm", "vert", None, None),
            P("tm", "vert", None),
            P("tm", "vert", None),
            P("tm", "vert", None, None),
        ),
        out_specs=P("tm", "vert", None),
        check_vma=False,
    )
```

profile of v0, /device:TPU:1, one launch (start us, length us, event | category | flops | bytes accessed | tf_op | source)
XLA Modules:
  0.0 263.2 jit_solution(4501448001142894589)
XLA Ops:
  10.4 84.7 %all-gather.3.cloned.1.call-done = bf16[1024,1024]{1,0:T(8,128)(2,1)} async-done(((bf16[32,1024]{1,0:T(8,128)(2,1)}), bf16[1024,1024]{1,0:T(8,128)(2,1)}) %all-gather.3.cloned.1.call-update) | async-done | bytes 2097168 | tf_op jit(solution)/shard_map/all_gather | solution.py:41
  95.1 2.8 %convolution_convert_fusion = bf16[512,1024]{1,0:T(8,128)(2,1)S(1)} fusion(bf16[1024,1024]{1,0:T(8,128)(2,1)} %all-gather.3.cloned.1.call-done, bf16[1,512,1024]{2,1,0:T(8,128)(2,1)S(1)} %copy-done), kind=kOutput, calls=%fused_computation.30 | convolution fusion | flops 1074266112 | bytes 4194304 | tf_op jit(solution)/shard_map/dot_general | solution.py:30
  97.9 2.1 gather_fusion
  101.2 5.9 %all-to-all-start = ((bf16[32,16,1024]{2,1,0:T(8,128)(2,1)}), bf16[32,16,1024]{2,1,0:T(8,128)(2,1)S(1)}, u32[]{:S(2)}, u32[]{:S(2)}) async-start(bf16[32,16,1024]{2,1,0:T(8,128)(2,1)} %select_select_fusion), calls=%async_computation | async-start | bytes 2097152 | tf_op jit(solution)/shard_map/all_to_all | solution.py:48
  107.4 19.0 %all-to-all-done = bf16[32,16,1024]{2,1,0:T(8,128)(2,1)S(1)} async-done(((bf16[32,16,1024]{2,1,0:T(8,128)(2,1)}), bf16[32,16,1024]{2,1,0:T(8,128)(2,1)S(1)}, u32[]{:S(2)}, u32[]{:S(2)}) %all-to-all-start) | async-done | bytes 1048608 | tf_op jit(solution)/shard_map/all_to_all | solution.py:48
  126.4 1.5 pad_maximum_fusion
  127.9 4.2 %gather_fusion.1 = bf16[12,128,1024]{2,1,0:T(8,128)(2,1)} fusion(bf16[8,128,1024]{2,1,0:T(8,128)(2,1)} %bitcast.57, s32[1024]{0:T(1024)S(1)} %pad_clamp_fusion), kind=kCustom, calls=%fused_computation.1 | custom fusion | bytes 6291504 | tf_op jit(solution)/shard_map/jit(_take)/gather | solution.py:57
  132.1 2.8 %fusion.4 = f32[4,1024,128,1]{1,2,3,0:T(8,128)S(1)} fusion(bf16[4,3,128,1024]{3,2,1,0:T(8,128)(2,1)} %bitcast.63, pred[4,3]{1,0:T(4,128)(4,1)S(1)} %compare_and_fusion.1, bf16[4,128,3,128]{3,1,0,2:T(8,128)(2,1)S(1)} %bitcast.67), kind=kOutput, calls=%fused_computation.9 | convolution fusion | flops 404226048 | bytes 5636108 | tf_op jit(solution)/shard_map/rikj,rkjd->rid/dot_general | solution.py:61
  135.3 3.0 %copy.63 = bf16[1,512,1024]{2,0,1:T(2,128)(2,1)} copy(bf16[1,512,1024]{2,1,0:T(8,128)(2,1)S(1)} %bitcast.58) | data formatting | bytes 2097152 | tf_op jit(solution)/shard_map/broadcast_in_dim | solution.py:64
  138.8 8.1 %reduce = bf16[512,1024]{1,0:T(8,128)(2,1)S(1)} reduce(bf16[512,1,1024]{2,1,0:T(2,128)(2,1)} %bitcast.60, bf16[]{:T(256)} %broadcast.92), dimensions={1}, to_apply=%bitcast.56.reduce_sub_computation | reduce | bytes 2097154
  146.9 1.6 reshape.151
  148.5 16.7 %all-to-all-start.1 = ((bf16[16,2,16384]{2,1,0:T(2,128)(2,1)}), bf16[16,2,16384]{2,1,0:T(2,128)(2,1)S(1)}, u32[]{:S(2)}, u32[]{:S(2)}) async-start(bf16[16,2,16384]{2,1,0:T(2,128)(2,1)} %reshape.151), calls=%async_computation.1 | async-start | bytes 2097152 | tf_op jit(solution)/shard_map/all_to_all | solution.py:64
  165.2 28.0 %all-to-all-done.1 = bf16[16,2,16384]{2,1,0:T(2,128)(2,1)S(1)} async-done(((bf16[16,2,16384]{2,1,0:T(2,128)(2,1)}), bf16[16,2,16384]{2,1,0:T(2,128)(2,1)S(1)}, u32[]{:S(2)}, u32[]{:S(2)}) %all-to-all-start.1) | async-done | bytes 1048608 | tf_op jit(solution)/shard_map/all_to_all | solution.py:64
  193.2 3.5 %reshape.152 = bf16[512,1,1024]{2,1,0:T(2,128)(2,1)} reshape(bf16[16,2,16384]{2,1,0:T(2,128)(2,1)S(1)} %all-to-all-done.1) | data formatting | bytes 2097152
  196.7 2.0 copy.51
  198.7 7.5 %fusion.7 = bf16[16,32,16,192]{3,1,2,0:T(8,128)(2,1)S(1)} fusion(bf16[16,32,1024,1]{2,1,3,0:T(8,128)(2,1)S(1)} %bitcast.64, bf16[16,192,1024]{2,1,0:T(8,128)(2,1)} %all-gather.5.cloned.1.call-done), kind=kOutput, calls=%fused_computation.12 | convolution fusion | flops 3222798336 | bytes 10485760 | tf_op jit(solution)/shard_map/tvd,hcd->tvhc/dot_general | solution.py:11
  206.3 1.8 fusion.32
  208.1 4.7 %fusion.15 = f32[32,16,16,16]{2,3,1,0:T(8,128)S(1)} fusion(bf16[16,32,16,64]{3,1,2,0:T(8,128)(2,1)S(1)} %get-tuple-element.6, bf16[16,32,16,64]{3,1,2,0:T(8,128)(2,1)S(1)} %get-tuple-element.7), kind=kOutput, calls=%fused_computation.21 | convolution fusion | flops 16777216 | bytes 2621440 | tf_op jit(solution)/shard_map/tvhc,svhc->vhts/dot_general | solution.py:15
  212.7 2.1 fusion.33
  214.8 3.2 %convert_bitcast_fusion = bf16[16,32,16,64]{3,0,2,1:T(8,128)(2,1)S(1)} fusion(f32[32,16,16,16]{2,3,1,0:T(8,128)S(1)} %get-tuple-element.9, f32[32,16,16]{2,1,0:T(8,128)S(1)} %get-tuple-element.8, bf16[16,32,16,64]{3,1,2,0:T(8,128)(2,1)S(1)} %get-tuple-element.5), kind=kOutput, calls=%fused_computation.24 | convolution fusion | flops 17563648 | bytes 2654208 | tf_op jit(solution)/shard_map/vhts,svhc->tvhc/dot_general | solution.py:23
  218.1 1.9 copy.47
  220.0 3.2 %reshape.129 = bf16[16,32,1024]{2,1,0:T(8,128)(2,1)S(1)} reshape(bf16[16,32,16,64]{3,2,1,0:T(8,128)(2,1)} %copy.47) | data formatting | bytes 2097152 | tf_op jit(solution)/shard_map/reshape | solution.py:24
  223.2 31.7 %all_to_all.26 = bf16[16,32,1024]{2,1,0:T(8,128)(2,1)S(1)} all-to-all(bf16[16,32,1024]{2,1,0:T(8,128)(2,1)S(1)} %reshape.129), channel_id=1, replica_groups=mesh['tm'=16,'vert'=32] {'tm'}, dimensions={0} | all-to-all | bytes 2097152 | tf_op jit(solution)/shard_map/all_to_all | solution.py:66
  254.9 1.4 fusion.25
  (27 shorter events, 6.2 us)
Async XLA Ops:
  6.5 88.6 %copy-start = (bf16[1,512,1024]{2,1,0:T(8,128)(2,1)S(1)}, bf16[1,512,1024]{2,1,0:T(8,128)(2,1)}, u32[]{:S(2)}) copy-start(bf16[1,512,1024]{2,1,0:T(8,128)(2,1)} %param.7) | copy-start | bytes 3145732
  6.5 88.5 %all-gather.3.cloned.1.call-start = ((), (), s32[]{:S(2)}) async-start(), calls=%async_computation.3 | async-start | bytes 2162688 | tf_op jit(solution)/shard_map/all_gather | solution.py:41
  7.3 191.5 %all-gather.5.cloned.1.call-start = ((), (), s32[]{:S(2)}) async-start(), calls=%async_computation.4 | async-start | bytes 6684672 | tf_op jit(solution)/shard_map/all_gather | solution.py:65
  100.0 7.1 %copy-start.1 = (s32[1,4,3]{1,0,2:T(1,128)S(1)}, s32[1,4,3]{1,0,2:T(1,128)}, u32[]{:S(2)}) copy-start(s32[1,4,3]{1,0,2:T(1,128)} %param.12) | copy-start | bytes 148
  101.2 25.2 %all-to-all-start = ((bf16[32,16,1024]{2,1,0:T(8,128)(2,1)}), bf16[32,16,1024]{2,1,0:T(8,128)(2,1)S(1)}, u32[]{:S(2)}, u32[]{:S(2)}) async-start(bf16[32,16,1024]{2,1,0:T(8,128)(2,1)} %select_select_fusion), calls=%async_computation | async-start | bytes 2097152 | tf_op jit(solution)/shard_map/all_to_all | solution.py:48
  127.9 4.2 %copy-start.2 = (bf16[1,512,3,128]{3,1,2,0:T(8,128)(2,1)S(1)}, bf16[1,512,3,128]{3,1,2,0:T(8,128)(2,1)}, u32[]{:S(2)}) copy-start(bf16[1,512,3,128]{3,1,2,0:T(8,128)(2,1)} %param.13) | copy-start | bytes 1179652
  148.5 44.7 %all-to-all-start.1 = ((bf16[16,2,16384]{2,1,0:T(2,128)(2,1)}), bf16[16,2,16384]{2,1,0:T(2,128)(2,1)S(1)}, u32[]{:S(2)}, u32[]{:S(2)}) async-start(bf16[16,2,16384]{2,1,0:T(2,128)(2,1)} %reshape.151), calls=%async_computation.1 | async-start | bytes 2097152 | tf_op jit(solution)/shard_map/all_to_all | solution.py:64
Sparse Core Ops, SparseCore 0:
  10.5 84.5 all-gather.2
  97.2 50.5 all-gather.4
where the time goes:
time: 264 us; the launch traced here: 263 us
  waiting for transfers between devices  133 us (50%)
  blocking collectives  31.7 us (12%)
  local copies, waits for them, and re-layouts  24.9 us (9%)
  starting transfers between devices  22.7 us (9%)
  matrix products  21 us (8%)
  other arithmetic  16.2 us (6%)
  between operations  13.5 us (5%)
    all_gather x1, waiting for transfers between devices, shards(): lax.all_gather(graph_weight, 'vert', axis=0, tiled=True)  84.7 us
    all_to_all x1, blocking collectives, shards(): lax.all_to_all(attended, 'tm', split_axis=0, concat_axis=1, tiled=True)  31.7 us
    all_to_all x1, waiting for transfers between devices, shards(): lax.all_to_all(hidden[None], 'tm', split_axis=1, concat_axis=0, tiled=True)  28 us
    all_to_all x1, waiting for transfers between devices, shards(): lax.all_to_all(picked, 'vert', split_axis=0, concat_axis=0, tiled=True)  19 us
    all_to_all x1, starting transfers between devices, shards(): lax.all_to_all(hidden[None], 'tm', split_axis=1, concat_axis=0, tiled=True)  16.7 us
    unnamed x12, local copies, waits for them, and re-layouts  8.44 us
    unnamed x1, other arithmetic  8.09 us
    dot_general x1, matrix products, attend_heads(): jnp.einsum('tvd,hcd->tvhc', regrouped, head_piece, preferred_element_type...  7.53 us
  transfers between devices with their start and end apart: 4, of which 3 were waited for; matrix products, arithmetic and copies ran while one was open for 14% of the time, Pallas kernels for 0%

commit v1 on v0

--- a/solution.py
+++ b/solution.py
@@ -61,7 +61,10 @@
     summed = jnp.einsum("rikj,rkjd->rid", edge_weights, chosen, preferred_element_type=jnp.float32)
     pre_act = projected.astype(jnp.float32) + summed.reshape(own_count, feature_width)
     hidden = jax.nn.relu(pre_act).astype(jnp.bfloat16)
-    regrouped = lax.all_to_all(hidden[None], "tm", split_axis=1, concat_axis=0, tiled=True)
+    regrouped = jnp.concatenate(
+        lax.all_to_all(jnp.stack(jnp.split(hidden[None], lax.axis_size("tm"), axis=1)), "tm", 0, 0),
+        axis=0,
+    )
     attended = attend_heads(regrouped, lax.all_gather(head_weight, "tm", axis=0, tiled=True))
     returned = lax.all_to_all(attended, "tm", split_axis=0, concat_axis=1, tiled=True)
     combined = (hidden.astype(jnp.float32) + returned[0].astype(jnp.float32)).astype(jnp.bfloat16)

time: 264 us -> 255 us (0.966)
  other arithmetic: 16.2 us -> 8.1 us
    unnamed x1 -> x0, other arithmetic: 8.09 us -> none
    broadcast_in_dim x1 -> x0, local copies, waits for them, and re-layouts: 2.96 us -> none  [shards(): hidden[None]]
    unnamed x12 -> x23, local copies, waits for them, and re-layouts: 8.44 us -> 10.4 us
  transfers between devices with their start and end apart: 4 -> 4, of which waited for: 3 -> 3; matrix products, arithmetic and copies ran while one was open for 14% -> 11% of each run, Pallas kernels for 0% -> 0%
where the time goes in v1:
time: 255 us
  waiting for transfers between devices  133 us (52%)
  blocking collectives  31.7 us (12%)
  local copies, waits for them, and re-layouts  24.5 us (10%)
  starting transfers between devices  22.6 us (9%)
  matrix products  21 us (8%)
  between operations  13.5 us (5%)
  other arithmetic  8.1 us (3%)
    all_gather x1, waiting for transfers between devices, shards(): lax.all_gather(graph_weight, 'vert', axis=0, tiled=True)  84.7 us
    all_to_all x1, blocking collectives, shards(): lax.all_to_all(attended, 'tm', split_axis=0, concat_axis=1, tiled=True)  31.7 us
    all_to_all x1, waiting for transfers between devices, shards(): lax.all_to_all(jnp.stack(jnp.split(hidden[None], lax.axis_size('tm'), axi...  28 us
    all_to_all x1, waiting for transfers between devices, shards(): lax.all_to_all(picked, 'vert', split_axis=0, concat_axis=0, tiled=True)  19.2 us
    all_to_all x1, starting transfers between devices, shards(): lax.all_to_all(jnp.stack(jnp.split(hidden[None], lax.axis_size('tm'), axi...  16.8 us
    unnamed x23, local copies, waits for them, and re-layouts  10.4 us
    dot_general x1, matrix products, attend_heads(): jnp.einsum('tvd,hcd->tvhc', regrouped, head_piece, preferred_element_type...  7.51 us
    all_to_all x1, starting transfers between devices, shards(): lax.all_to_all(picked, 'vert', split_axis=0, concat_axis=0, tiled=True)  5.74 us
  transfers between devices with their start and end apart: 4, of which 3 were waited for; matrix products, arithmetic and copies ran while one was open for 11% of the time, Pallas kernels for 0%

profile of v1, /device:TPU:1, one launch (start us, length us, event | category | flops | bytes accessed | tf_op | source)
XLA Modules:
  0.0 254.6 jit_solution(89406956544368100)
XLA Ops:
  6.5 0.7 all-gather.3.cloned.1.call-update
  8.0 0.8 copy.28
  8.9 0.7 compare_and_fusion
  9.7 0.7 iota_compare_fusion
  10.4 84.7 %all-gather.3.cloned.1.call-done = bf16[1024,1024]{1,0:T(8,128)(2,1)} async-done(((bf16[32,1024]{1,0:T(8,128)(2,1)}), bf16[1024,1024]{1,0:T(8,128)(2,1)}) %all-gather.3.cloned.1.call-update) | async-done | bytes 2097168 | tf_op jit(solution)/shard_map/all_gather | solution.py:41
  95.1 2.8 %convolution_convert_fusion = bf16[512,1024]{1,0:T(8,128)(2,1)S(1)} fusion(bf16[1024,1024]{1,0:T(8,128)(2,1)} %all-gather.3.cloned.1.call-done, bf16[1,512,1024]{2,1,0:T(8,128)(2,1)S(1)} %copy-done), kind=kOutput, calls=%fused_computation.30 | convolution fusion | flops 1074266112 | bytes 4194304 | tf_op jit(solution)/shard_map/dot_general | solution.py:30
  97.9 2.1 gather_fusion
  100.0 1.2 select_select_fusion
  101.2 5.7 %all-to-all-start = ((bf16[32,16,1024]{2,1,0:T(8,128)(2,1)}), bf16[32,16,1024]{2,1,0:T(8,128)(2,1)S(1)}, u32[]{:S(2)}, u32[]{:S(2)}) async-start(bf16[32,16,1024]{2,1,0:T(8,128)(2,1)} %select_select_fusion), calls=%async_computation | async-start | bytes 2097152 | tf_op jit(solution)/shard_map/all_to_all | solution.py:48
  107.2 19.2 %all-to-all-done = bf16[32,16,1024]{2,1,0:T(8,128)(2,1)S(1)} async-done(((bf16[32,16,1024]{2,1,0:T(8,128)(2,1)}), bf16[32,16,1024]{2,1,0:T(8,128)(2,1)S(1)}, u32[]{:S(2)}, u32[]{:S(2)}) %all-to-all-start) | async-done | bytes 1048608 | tf_op jit(solution)/shard_map/all_to_all | solution.py:48
  126.4 1.5 pad_maximum_fusion
  127.9 4.2 %gather_fusion.1 = bf16[12,128,1024]{2,1,0:T(8,128)(2,1)} fusion(bf16[8,128,1024]{2,1,0:T(8,128)(2,1)} %bitcast.119, s32[1024]{0:T(1024)S(1)} %pad_clamp_fusion), kind=kCustom, calls=%fused_computation.1 | custom fusion | bytes 6291504 | tf_op jit(solution)/shard_map/jit(_take)/gather | solution.py:57
  132.1 2.8 %fusion.4 = f32[4,1024,128,1]{1,2,3,0:T(8,128)S(1)} fusion(bf16[4,3,128,1024]{3,2,1,0:T(8,128)(2,1)} %bitcast.138, pred[4,3]{1,0:T(4,128)(4,1)S(1)} %compare_and_fusion.1, bf16[4,128,3,128]{3,1,0,2:T(8,128)(2,1)S(1)} %bitcast.141), kind=kOutput, calls=%fused_computation.9 | convolution fusion | flops 404226048 | bytes 5636108 | tf_op jit(solution)/shard_map/rikj,rkjd->rid/dot_general | solution.py:61
  145.5 16.8 %all-to-all-start.1 = ((bf16[16,1,32,1024]{3,2,1,0:T(8,128)(2,1)}), bf16[16,1,32,1024]{3,2,1,0:T(8,128)(2,1)S(1)}, u32[]{:S(2)}, u32[]{:S(2)}) async-start(bf16[16,1,32,1024]{3,2,1,0:T(8,128)(2,1)} %fusion.29), calls=%async_computation.1 | async-start | bytes 2097152 | tf_op jit(solution)/shard_map/all_to_all | solution.py:65
  162.3 28.0 %all-to-all-done.1 = bf16[16,1,32,1024]{3,2,1,0:T(8,128)(2,1)S(1)} async-done(((bf16[16,1,32,1024]{3,2,1,0:T(8,128)(2,1)}), bf16[16,1,32,1024]{3,2,1,0:T(8,128)(2,1)S(1)}, u32[]{:S(2)}, u32[]{:S(2)}) %all-to-all-start.1) | async-done | bytes 1048608 | tf_op jit(solution)/shard_map/all_to_all | solution.py:65
  190.3 7.5 %fusion.7 = bf16[16,32,16,192]{3,1,2,0:T(8,128)(2,1)S(1)} fusion(bf16[16,192,1024]{2,1,0:T(8,128)(2,1)} %all-gather.5.cloned.1.call-done, bf16[16,1,32,1024]{3,2,1,0:T(8,128)(2,1)S(1)} %all-to-all-done.1), kind=kOutput, calls=%fused_computation.12 | convolution fusion | flops 3222798336 | bytes 10485760 | tf_op jit(solution)/shard_map/tvd,hcd->tvhc/dot_general | solution.py:11
  197.8 1.8 fusion.49
  199.6 4.7 %fusion.15 = f32[32,16,16,16]{2,3,1,0:T(8,128)S(1)} fusion(bf16[16,32,16,64]{3,1,2,0:T(8,128)(2,1)S(1)} %get-tuple-element.6, bf16[16,32,16,64]{3,1,2,0:T(8,128)(2,1)S(1)} %get-tuple-element.7), kind=kOutput, calls=%fused_computation.21 | convolution fusion | flops 16777216 | bytes 2621440 | tf_op jit(solution)/shard_map/tvhc,svhc->vhts/dot_general | solution.py:15
  204.2 2.1 fusion.50
  206.4 3.2 %convert_bitcast_fusion = bf16[16,32,16,64]{3,0,2,1:T(8,128)(2,1)S(1)} fusion(f32[32,16,16,16]{2,3,1,0:T(8,128)S(1)} %get-tuple-element.9, f32[32,16,16]{2,1,0:T(8,128)S(1)} %get-tuple-element.8, bf16[16,32,16,64]{3,1,2,0:T(8,128)(2,1)S(1)} %get-tuple-element.5), kind=kOutput, calls=%fused_computation.24 | convolution fusion | flops 17563648 | bytes 2654208 | tf_op jit(solution)/shard_map/vhts,svhc->tvhc/dot_general | solution.py:23
  209.6 1.9 copy.35
  211.5 3.2 %reshape.130 = bf16[16,32,1024]{2,1,0:T(8,128)(2,1)S(1)} reshape(bf16[16,32,16,64]{3,2,1,0:T(8,128)(2,1)} %copy.35) | data formatting | bytes 2097152 | tf_op jit(solution)/shard_map/reshape | solution.py:24
  214.7 31.7 %all_to_all.19 = bf16[16,32,1024]{2,1,0:T(8,128)(2,1)S(1)} all-to-all(bf16[16,32,1024]{2,1,0:T(8,128)(2,1)S(1)} %reshape.130), channel_id=1, replica_groups=mesh['tm'=16,'vert'=32] {'tm'}, dimensions={0} | all-to-all | bytes 2097152 | tf_op jit(solution)/shard_map/all_to_all | solution.py:69
  246.4 1.4 fusion.25
  (37 shorter events, 11.7 us)
Async XLA Ops:
  6.5 88.6 %copy-start = (bf16[1,512,1024]{2,1,0:T(8,128)(2,1)S(1)}, bf16[1,512,1024]{2,1,0:T(8,128)(2,1)}, u32[]{:S(2)}) copy-start(bf16[1,512,1024]{2,1,0:T(8,128)(2,1)} %param.7) | copy-start | bytes 3145732
  6.5 88.5 %all-gather.3.cloned.1.call-start = ((), (), s32[]{:S(2)}) async-start(), calls=%async_computation.3 | async-start | bytes 2162688 | tf_op jit(solution)/shard_map/all_gather | solution.py:41
  7.3 183.0 %all-gather.5.cloned.1.call-start = ((), (), s32[]{:S(2)}) async-start(), calls=%async_computation.4 | async-start | bytes 6684672 | tf_op jit(solution)/shard_map/all_gather | solution.py:68
  100.0 7.0 %copy-start.1 = (s32[1,4,3]{1,0,2:T(1,128)S(1)}, s32[1,4,3]{1,0,2:T(1,128)}, u32[]{:S(2)}) copy-start(s32[1,4,3]{1,0,2:T(1,128)} %param.12) | copy-start | bytes 148
  101.2 25.2 %all-to-all-start = ((bf16[32,16,1024]{2,1,0:T(8,128)(2,1)}), bf16[32,16,1024]{2,1,0:T(8,128)(2,1)S(1)}, u32[]{:S(2)}, u32[]{:S(2)}) async-start(bf16[32,16,1024]{2,1,0:T(8,128)(2,1)} %select_select_fusion), calls=%async_computation | async-start | bytes 2097152 | tf_op jit(solution)/shard_map/all_to_all | solution.py:48
  127.9 4.2 %copy-start.2 = (bf16[1,512,3,128]{3,1,2,0:T(8,128)(2,1)S(1)}, bf16[1,512,3,128]{3,1,2,0:T(8,128)(2,1)}, u32[]{:S(2)}) copy-start(bf16[1,512,3,128]{3,1,2,0:T(8,128)(2,1)} %param.13) | copy-start | bytes 1179652
  145.5 44.8 %all-to-all-start.1 = ((bf16[16,1,32,1024]{3,2,1,0:T(8,128)(2,1)}), bf16[16,1,32,1024]{3,2,1,0:T(8,128)(2,1)S(1)}, u32[]{:S(2)}, u32[]{:S(2)}) async-start(bf16[16,1,32,1024]{3,2,1,0:T(8,128)(2,1)} %fusion.29), calls=%async_computation.1 | async-start | bytes 2097152 | tf_op jit(solution)/shard_map/all_to_all | solution.py:65
Sparse Core Ops, SparseCore 0:
  10.5 84.5 all-gather.2
  97.2 50.5 all-gather.4
